TPU v7x, 128 devices: a whole 4x4x4 slice. The times are simulated.
128 devices in a mesh: leaf: 16 (over x, y_lo, core), panel: 8 (over z, y_hi).
Axes of the slice: x: 4, y: 4 (y_hi: 2, y_lo: 2; y = y_hi * 2 + y_lo), z: 4, core: 2. Of those that a mesh axis runs over, the one named last changes fastest.
Arguments:
- ext_rows: bfloat16 [16, 4608, 5120], P('leaf', 'panel'), as said below
- iface_rows: bfloat16 [16, 512, 5120], P('leaf', 'panel'), as said below
- inverse: bfloat16 [16, 512, 512], P('leaf', 'panel'), as said below
- pivot: int32 [16, 256], P('leaf'), may hold values from 0 to 255, as said below
- flags: int32 [16, 9], P('leaf'), may hold values 0 or 1
Outputs:
- merged: bfloat16 [16, 4608, 9216], P('leaf', 'panel')
Inputs may be any that keep to these rules, and one draw needn't show every extreme that they name: `pivot`: each row is a permutation of 0 to 255; the rows of two merge partners are inverse to each other. `ext_rows`: each 2 x 2 block of real entries is the real form [[a, -b], [b, a]] of one complex number. `iface_rows`: each 2 x 2 block of real entries is the real form [[a, -b], [b, a]] of one complex number. `inverse`: each 2 x 2 block of real entries is the real form [[a, -b], [b, a]] of one complex number.
All inputs are finite; a program needn't handle non-finite values. No bound on the sum of `flags` on one device may be relied on, other than what follows from the above.
Results may differ from a plain program's by a relative error of at most 0.005.
Values may be sent and summed in bfloat16 or wider, within the bound.
No kernel may reach another device: no remote copies, remote signals or barrier semaphores. Data moves between devices by JAX's collectives and lax.ppermute only.
A program may use at most 128 MiB of HBM per device.

v0:
```python
import jax
import jax.numpy as jnp
from jax import lax
from jax.sharding import PartitionSpec as P

FPTS = 256
BIT = 2


def partner(array, axis, bit):
    return lax.ppermute(array, axis, [(i, i ^ 1 << bit) for i in range(lax.axis_size(axis))])


def per_device(ext_rows, iface_rows, inverse, pivot, flags):
    ext = ext_rows[0]
    iface = iface_rows[0]
    winv = inverse[0]
    idim = winv.shape[1]
    edim = ext.shape[1] - idim
    rows = ext.shape[0]
    direct_block = ext[:, :edim]
    ext_to_iface = ext[:, edim:]
    own_outward = iface[:, :edim]
    own_inward = iface[:, edim:]
    order = (2 * pivot[0][:, None] + jnp.arange(2, dtype=jnp.int32)[None, :]).reshape(-1)
    back = jnp.argsort(order)
    permuted = jnp.take(winv, back, axis=1)
    coupled = jnp.dot(
        ext_to_iface,
        lax.all_gather(permuted, "panel", axis=0, tiled=True),
        preferred_element_type=jnp.float32,
    ).astype(jnp.bfloat16)
    inward_send = lax.all_gather(own_inward, "panel", axis=0, tiled=True)
    partner_inward, partner_outward = partner((inward_send, own_outward), "leaf", BIT)
    through = jnp.dot(
        coupled, jnp.take(partner_inward, order, axis=1), preferred_element_type=jnp.float32
    )
    through = through.astype(jnp.bfloat16)
    own_sum = jnp.dot(
        through,
        lax.all_gather(own_outward, "panel", axis=0, tiled=True),
        preferred_element_type=jnp.float32,
    )
    cross_sum = jnp.dot(
        coupled,
        lax.all_gather(partner_outward, "panel", axis=0, tiled=True),
        preferred_element_type=jnp.float32,
    )
    cross = cross_sum.astype(jnp.bfloat16)
    own = direct_block.astype(jnp.float32) + own_sum
    row_index = lax.axis_index("panel") * rows + jnp.arange(rows, dtype=jnp.int32)
    face_index = row_index // (2 * FPTS)
    faces = flags.shape[1]
    matches = (face_index[:, None] == jnp.arange(faces, dtype=jnp.int32)[None, :]).astype(
        jnp.float32
    )
    opened = jnp.sum(matches * flags[0][None, :].astype(jnp.float32), axis=1)
    sign = 1.0 - 2.0 * opened
    whole = jnp.concatenate([own, cross.astype(jnp.float32)], axis=1)
    return (sign[:, None] * whole).astype(jnp.bfloat16)[None]


def solution(mesh):
    placed = (
        P("leaf", "panel", None),
        P("leaf", "panel", None),
        P("leaf", "panel", None),
        P("leaf", None),
        P("leaf", None),
    )
    return jax.shard_map(
        per_device, mesh=mesh, in_specs=placed, out_specs=P("leaf", "panel", None), check_vma=False
    )
```

profile of v0, /device:TPU:0, one launch (start us, length us, event | category | flops | bytes accessed | tf_op | source)
XLA Modules:
  0.0 188.1 jit_solution(17509091723812896710)
XLA Ops:
  6.5 0.0 all-gather.3.cloned.1.call-start
  6.5 1.9 %slice.23 = bf16[64,4608]{1,0:T(8,128)(2,1)} slice(bf16[64,5120]{1,0:T(8,128)(2,1)} %bitcast.22), slice={[0:64], [0:4608]} | slice | bytes 1179648 | tf_op jit(solution)/shard_map/slice | solution.py:23
  8.5 0.0 all-gather.3.cloned.1.call-update
  8.5 0.0 all-gather.5.cloned.1.call-start
  8.5 1.7 collective-permute-start.1
  10.2 13.5 %collective-permute-done.1 = bf16[64,4608]{1,0:T(8,128)(2,1)S(1)} collective-permute-done((bf16[64,4608]{1,0:T(8,128)(2,1)}, bf16[64,4608]{1,0:T(8,128)(2,1)S(1)}, u32[]{:S(2)}, u32[]{:S(2)}) %collective-permute-start.1) | collective-permute-done | bytes 589856 | tf_op jit(solution)/shard_map/ppermute | solution.py:11
  23.7 0.0 copy-start.1
  23.7 0.8 copy-done.1
  24.6 0.0 all-gather.5.cloned.1.call-update
  24.6 0.8 slice.22
  25.4 39.8 %all_gather.13 = bf16[512,512]{1,0:T(8,128)(2,1)S(1)} all-gather(bf16[64,512]{1,0:T(8,128)(2,1)S(1)} %slice.22), channel_id=1, replica_groups=mesh['leaf'=16,'panel'=8] {'panel'}, dimensions={0}, use_global_device_ids=true | all-gather | bytes 589824 | tf_op jit(solution)/shard_map/all_gather | solution.py:33
  65.2 0.2 copy.15
  65.4 1.6 collective-permute-start
  67.0 0.7 broadcast_multiply_fusion
  67.7 0.1 iota_add_fusion
  67.8 0.1 add.79
  67.9 0.1 add.83
  68.0 1.0 copy.13
  69.0 3.8 %sort.17 = (s32[512]{0:T(512)}, s32[512]{0:T(512)S(1)}) sort(s32[512]{0:T(512)S(1)} %add.79, s32[512]{0:T(512)S(1)} %iota.18), dimensions={0}, to_apply=%region_1.2 | sort | flops 4608 | bytes 8192 | tf_op jit(solution)/shard_map/jit(argsort)/sort | solution.py:26
  72.8 1.3 gather_fusion
  74.2 0.7 convert_bitcast_fusion
  74.8 0.1 select_reduce_fusion
  75.0 0.1 select_bitcast_fusion
  75.1 0.1 copy.14
  75.2 36.9 %all_gather.12 = bf16[512,512]{1,0:T(8,128)(2,1)S(1)} all-gather(bf16[64,512]{1,0:T(8,128)(2,1)S(1)} %copy.14), channel_id=1, replica_groups=mesh['leaf'=16,'panel'=8] {'panel'}, dimensions={0}, use_global_device_ids=true | all-gather | bytes 589824 | tf_op jit(solution)/shard_map/all_gather | solution.py:30
  112.1 1.5 convolution_convert_fusion.1
  113.7 0.0 collective-permute-done
  113.7 2.0 %gather_fusion.1 = bf16[512,512]{1,0:T(8,128)(2,1)S(1)} fusion(bf16[512,512]{0,1:T(8,128)(2,1)S(1)} %collective-permute-done, s32[1024]{0:T(1024)S(1)} %pad_clamp_fusion), kind=kCustom, calls=%fused_computation.1 | custom fusion | bytes 1050624 | tf_op jit(solution)/shard_map/jit(_take)/gather | solution.py:36
  115.6 0.0 all-gather.3.cloned.1.call-done
  115.7 9.3 %add_bitcast_fusion = f32[1,576,4608]{2,1,0:T(8,128)} fusion(bf16[512,4608]{1,0:T(8,128)(2,1)} %all-gather.3.cloned.1.call-done, bf16[576,5120]{1,0:T(8,128)(2,1)} %bitcast.27, bf16[512,576]{0,1:T(8,128)(2,1)S(1)} %convolution_convert_fusion.1, bf16[512,512]{1,0:T(8,128)(2,1)S(1)} %gather_fusion.1, pred[512]{0:T(512)(128)(4,1)S(1)} %compare_and_fusion), kind=kOutput, calls=%fused_computation.4 | convolution fusion | flops 3025764352 | bytes 21758464 | tf_op jit(solution)/shard_map/dot_general | solution.py:39
  125.0 45.7 %all-gather.5.cloned.1.call-done = bf16[512,4608]{1,0:T(8,128)(2,1)} async-done(((bf16[64,4608]{1,0:T(8,128)(2,1)}), bf16[512,4608]{1,0:T(8,128)(2,1)}) %all-gather.5.cloned.1.call-update) | async-done | bytes 4718608 | tf_op jit(solution)/shard_map/all_gather | solution.py:46
  170.7 0.0 copy-start
  170.7 4.9 %fusion.2 = f32[1,576,4608]{2,1,0:T(8,128)S(1)} fusion(bf16[512,576]{0,1:T(8,128)(2,1)S(1)} %convolution_convert_fusion.1, bf16[512,4608]{1,0:T(8,128)(2,1)} %all-gather.5.cloned.1.call-done), kind=kOutput, calls=%fused_computation.7 | convolution fusion | flops 2723217408 | bytes 15925248 | tf_op jit(solution)/shard_map/dot_general | solution.py:44
  175.7 0.5 copy-done
  176.1 5.1 %fusion = bf16[1,576,9216]{2,1,0:T(8,128)(2,1)} fusion(f32[1,576,4608]{2,1,0:T(8,128)S(1)} %fusion.2, f32[1,576,4608]{2,1,0:T(8,128)S(1)} %copy-done, f32[576]{0:T(1024)S(1)} %multiply_subtract_fusion), kind=kLoop, calls=%fused_computation.3 | loop fusion | flops 15925248 | bytes 31852800 | tf_op jit(solution)/shard_map/convert_element_type | solution.py:60
  (9 shorter events, 0.1 us)
Async XLA Ops:
  6.5 109.1 %all-gather.3.cloned.1.call-start = ((), (), s32[]{:S(2)}) async-start(), calls=%async_computation | async-start | bytes 5308416 | tf_op jit(solution)/shard_map/all_gather | solution.py:41
  8.5 162.2 %all-gather.5.cloned.1.call-start = ((), (), s32[]{:S(2)}) async-start(), calls=%async_computation.1 | async-start | bytes 5308416 | tf_op jit(solution)/shard_map/all_gather | solution.py:46
  8.5 15.2 %collective-permute-start.1 = (bf16[64,4608]{1,0:T(8,128)(2,1)}, bf16[64,4608]{1,0:T(8,128)(2,1)S(1)}, u32[]{:S(2)}, u32[]{:S(2)}) collective-permute-start(bf16[64,4608]{1,0:T(8,128)(2,1)} %slice.23), channel_id=1, source_target_pairs={{0,32},{8,40},{16,48},{24,56},{32,0},{40,8},{48,16},{56,24},{64,96... | collective-permute-start | bytes 1769480 | tf_op jit(solution)/shard_map/ppermute | solution.py:11
  23.7 0.8 copy-start.1
  65.4 48.3 %collective-permute-start = (bf16[512,512]{0,1:T(8,128)(2,1)S(1)}, bf16[512,512]{0,1:T(8,128)(2,1)S(1)}, u32[]{:S(2)}, u32[]{:S(2)}) collective-permute-start(bf16[512,512]{0,1:T(8,128)(2,1)S(1)} %copy.15), channel_id=1, source_target_pairs={{0,32},{8,40},{16,48},{24,56},{32,0},{40,8},{48,16},{56,24},{64,96... | collective-permute-start | bytes 1572872 | tf_op jit(solution)/shard_map/ppermute | solution.py:11
  170.7 5.4 %copy-start = (f32[1,576,4608]{2,1,0:T(8,128)S(1)}, f32[1,576,4608]{2,1,0:T(8,128)}, u32[]{:S(2)}) copy-start(f32[1,576,4608]{2,1,0:T(8,128)} %add_bitcast_fusion) | copy-start | bytes 31850500
Sparse Core Ops, SparseCore 0:
  9.6 84.3 all-gather.2
  96.3 74.3 all-gather.4
where the time goes:
time: 188 us
  blocking collectives  76.6 us (41%)
  waiting for transfers between devices  59.3 us (32%)
  matrix products  15.8 us (8%)
  between operations  13.5 us (7%)
  other arithmetic  10.6 us (6%)
  local copies, waits for them, and re-layouts  8.93 us (5%)
  starting transfers between devices  3.29 us (2%)
    all_gather x1, waiting for transfers between devices, per_device(): lax.all_gather(partner_outward, 'panel', axis=0, tiled=True)  45.7 us
    all_gather x1, blocking collectives, per_device(): inward_send = lax.all_gather(own_inward, 'panel', axis=0, tiled=True)  39.8 us
    all_gather x1, blocking collectives, per_device(): lax.all_gather(permuted, 'panel', axis=0, tiled=True)  36.9 us
    ppermute x2, waiting for transfers between devices, partner(): lax.ppermute(array, axis, [(i, i ^ 1 << bit) for i in range(lax.axis_size...  13.5 us
    dot_general x1, matrix products, per_device(): jnp.dot(through, lax.all_gather(own_outward, 'panel', axis=0, tiled=True)...  9.34 us
    convert_element_type x1, other arithmetic, per_device(): return (sign[:, None] * whole).astype(jnp.bfloat16)[None]  5.09 us
    dot_general x1, matrix products, per_device(): jnp.dot(coupled, lax.all_gather(partner_outward, 'panel', axis=0, tiled=T...  4.93 us
    sort x1, other arithmetic, per_device(): back = jnp.argsort(order)  3.78 us
  transfers between devices with their start and end apart: 4, of which 2 were waited for; matrix products, arithmetic and copies ran while one was open for 12% of the time, Pallas kernels for 0%

commit v1 on v0

--- a/solution.py
+++ b/solution.py
@@ -43,7 +43,10 @@
     )
     cross_sum = jnp.dot(
         coupled,
-        lax.all_gather(partner_outward, "panel", axis=0, tiled=True),
+        jnp.concatenate(
+            lax.all_to_all(jnp.stack([partner_outward] * lax.axis_size("panel")), "panel", 0, 0),
+            axis=0,
+        ),
         preferred_element_type=jnp.float32,
     )
     cross = cross_sum.astype(jnp.bfloat16)

time: 188 us -> 228 us (1.21)
  blocking collectives: 76.6 us -> 145 us
  waiting for transfers between devices: 59.3 us -> 13.6 us
  starting transfers between devices: 3.29 us -> 11.6 us
  other arithmetic: 10.6 us -> 16.1 us
  matrix products: 15.8 us -> 18.6 us
    all_gather x1, blocking collectives: 39.8 us -> 110 us  [per_device(): inward_send = lax.all_gather(own_inward, 'panel', axis=0, tiled=True)]
    all_gather x1 -> x0, waiting for transfers between devices: 45.7 us -> none  [per_device(): lax.all_gather(partner_outward, 'panel', axis=0, tiled=True)]
    all_to_all x0 -> x1, starting transfers between devices: none -> 8.33 us  [per_device(): lax.all_to_all(jnp.stack([partner_outward] * lax.axis_size('panel')), 'pa...]
    convert_element_type x1, other arithmetic: 5.09 us -> 11.9 us  [per_device(): return (sign[:, None] * whole).astype(jnp.bfloat16)[None]]
    dot_general x1, matrix products: 4.93 us -> 7.91 us  [per_device(): jnp.dot(coupled, jnp.concatenate(lax.all_to_all(jnp.stack([partner_outwar...]
    another operation x0 -> x1, local copies, waits for them, and re-layouts: none -> 2.57 us  [per_device(): jnp.stack([partner_outward] * lax.axis_size('panel'))]
  transfers between devices with their start and end apart: 4 -> 4, of which waited for: 2 -> 1; matrix products, arithmetic and copies ran while one was open for 12% -> 9% of each run, Pallas kernels for 0% -> 0%
where the time goes in v1:
time: 228 us
  blocking collectives  145 us (64%)
  matrix products  18.6 us (8%)
  other arithmetic  16.1 us (7%)
  waiting for transfers between devices  13.6 us (6%)
  between operations  13.6 us (6%)
  starting transfers between devices  11.6 us (5%)
  local copies, waits for them, and re-layouts  9.37 us (4%)
    all_gather x1, blocking collectives, per_device(): inward_send = lax.all_gather(own_inward, 'panel', axis=0, tiled=True)  110 us
    all_gather x1, blocking collectives, per_device(): lax.all_gather(permuted, 'panel', axis=0, tiled=True)  35.4 us
    ppermute x2, waiting for transfers between devices, partner(): lax.ppermute(array, axis, [(i, i ^ 1 << bit) for i in range(lax.axis_size...  13.5 us
    convert_element_type x1, other arithmetic, per_device(): return (sign[:, None] * whole).astype(jnp.bfloat16)[None]  11.9 us
    dot_general x1, matrix products, per_device(): jnp.dot(through, lax.all_gather(own_outward, 'panel', axis=0, tiled=True)...  9.18 us
    all_to_all x1, starting transfers between devices, per_device(): lax.all_to_all(jnp.stack([partner_outward] * lax.axis_size('panel')), 'pa...  8.33 us
    dot_general x1, matrix products, per_device(): jnp.dot(coupled, jnp.concatenate(lax.all_to_all(jnp.stack([partner_outwar...  7.91 us
  transfers between devices with their start and end apart: 4, of which 1 were waited for; matrix products, arithmetic and copies ran while one was open for 9% of the time, Pallas kernels for 0%

profile of v1, /device:TPU:0, one launch (start us, length us, event | category | flops | bytes accessed | tf_op | source)
XLA Modules:
  0.0 227.8 jit_solution(5612745478613453591)
XLA Ops:
  6.5 0.0 all-gather.2.cloned.1.call-start
  6.5 1.9 slice.23
  8.5 0.0 all-gather.2.cloned.1.call-update
  8.5 1.7 collective-permute-start.1
  10.2 13.5 %collective-permute-done.1 = bf16[64,4608]{1,0:T(8,128)(2,1)S(1)} collective-permute-done((bf16[64,4608]{1,0:T(8,128)(2,1)}, bf16[64,4608]{1,0:T(8,128)(2,1)S(1)}, u32[]{:S(2)}, u32[]{:S(2)}) %collective-permute-start.1) | collective-permute-done | bytes 589856 | tf_op jit(solution)/shard_map/ppermute | solution.py:11
  23.7 2.6 %stack.2 = bf16[8,64,4608]{2,1,0:T(8,128)(2,1)} broadcast(bf16[64,4608]{1,0:T(8,128)(2,1)S(1)} %collective-permute-done.1), dimensions={1,2} | broadcast | bytes 5308416 | tf_op jit(solution)/shard_map/stack | solution.py:47
  26.3 0.0 copy-start.1
  26.3 0.0 copy-start
  26.3 0.0 copy-start.2
  26.3 8.3 %all-to-all-start = ((bf16[8,64,4608]{2,1,0:T(8,128)(2,1)}), bf16[8,64,4608]{2,1,0:T(8,128)(2,1)}, u32[]{:S(2)}, u32[]{:S(2)}) async-start(bf16[8,64,4608]{2,1,0:T(8,128)(2,1)} %stack.2), calls=%async_computation | async-start | bytes 9437184 | tf_op jit(solution)/shard_map/all_to_all | solution.py:47
  34.6 0.8 slice.22
  35.5 109.7 %all_gather.10 = bf16[512,512]{1,0:T(8,128)(2,1)S(1)} all-gather(bf16[64,512]{1,0:T(8,128)(2,1)S(1)} %slice.22), channel_id=1, replica_groups=mesh['leaf'=16,'panel'=8] {'panel'}, dimensions={0}, use_global_device_ids=true | all-gather | bytes 589824 | tf_op jit(solution)/shard_map/all_gather | solution.py:33
  145.1 0.2 copy.17
  145.4 1.6 collective-permute-start
  147.0 0.0 copy-done.1
  147.0 0.1 iota_add_fusion
  147.1 0.1 add.79
  147.2 0.1 add.83
  147.4 0.0 copy-done
  147.4 0.1 copy.15
  147.5 3.8 %sort.17 = (s32[512]{0:T(512)}, s32[512]{0:T(512)S(1)}) sort(s32[512]{0:T(512)S(1)} %add.79, s32[512]{0:T(512)S(1)} %iota.18), dimensions={0}, to_apply=%region_1.2 | sort | flops 4608 | bytes 8192 | tf_op jit(solution)/shard_map/jit(argsort)/sort | solution.py:26
  151.3 1.3 gather_fusion
  152.6 0.0 copy-done.2
  152.7 0.1 select_reduce_fusion
  152.8 0.1 select_bitcast_fusion
  153.0 0.1 copy.16
  153.1 35.4 %all_gather.9 = bf16[512,512]{1,0:T(8,128)(2,1)S(1)} all-gather(bf16[64,512]{1,0:T(8,128)(2,1)S(1)} %copy.16), channel_id=1, replica_groups=mesh['leaf'=16,'panel'=8] {'panel'}, dimensions={0}, use_global_device_ids=true | all-gather | bytes 589824 | tf_op jit(solution)/shard_map/all_gather | solution.py:30
  188.4 1.5 convolution_convert_fusion.1
  190.0 0.0 collective-permute-done
  190.0 2.0 gather_fusion.1
  192.0 0.0 all-to-all-done
  192.0 7.9 %fusion.2 = f32[1,576,4608]{2,1,0:T(8,128)} fusion(bf16[512,576]{0,1:T(8,128)(2,1)S(1)} %convolution_convert_fusion.1, bf16[512,4608]{1,0:T(8,128)(2,1)} %bitcast.8), kind=kOutput, calls=%fused_computation.7 | convolution fusion | flops 2723217408 | bytes 15925248 | tf_op jit(solution)/shard_map/dot_general | solution.py:44
  199.9 0.0 all-gather.2.cloned.1.call-done
  199.9 9.2 %add_bitcast_fusion = f32[1,576,4608]{2,1,0:T(8,128)} fusion(bf16[512,4608]{1,0:T(8,128)(2,1)} %all-gather.2.cloned.1.call-done, bf16[576,5120]{1,0:T(8,128)(2,1)} %bitcast.28, bf16[512,576]{0,1:T(8,128)(2,1)S(1)} %convolution_convert_fusion.1, bf16[512,512]{1,0:T(8,128)(2,1)S(1)} %gather_fusion.1, pred[512]{0:T(512)(128)(4,1)S(1)} %compare_and_fusion), kind=kOutput, calls=%fused_computation.4 | convolution fusion | flops 3025764352 | bytes 21758464 | tf_op jit(solution)/shard_map/dot_general | solution.py:39
  209.1 11.9 %fusion = bf16[1,576,9216]{2,1,0:T(8,128)(2,1)} fusion(f32[1,576,4608]{2,1,0:T(8,128)} %fusion.2, f32[1,576,4608]{2,1,0:T(8,128)} %add_bitcast_fusion, f32[576]{0:T(1024)S(1)} %multiply_subtract_fusion), kind=kLoop, calls=%fused_computation.3 | loop fusion | flops 15925248 | bytes 31852800 | tf_op jit(solution)/shard_map/convert_element_type | solution.py:63
  (11 shorter events, 0.1 us)
Async XLA Ops:
  6.5 193.4 %all-gather.2.cloned.1.call-start = ((), (), s32[]{:S(2)}) async-start(), calls=%async_computation.1 | async-start | bytes 5308416 | tf_op jit(solution)/shard_map/all_gather | solution.py:41
  8.5 15.2 %collective-permute-start.1 = (bf16[64,4608]{1,0:T(8,128)(2,1)}, bf16[64,4608]{1,0:T(8,128)(2,1)S(1)}, u32[]{:S(2)}, u32[]{:S(2)}) collective-permute-start(bf16[64,4608]{1,0:T(8,128)(2,1)} %slice.23), channel_id=1, source_target_pairs={{0,32},{8,40},{16,48},{24,56},{32,0},{40,8},{48,16},{56,24},{64,96... | collective-permute-start | bytes 1769480 | tf_op jit(solution)/shard_map/ppermute | solution.py:11
  26.3 120.7 %copy-start.1 = (s32[1,256]{1,0:T(1,128)S(1)}, s32[1,256]{1,0:T(1,128)}, u32[]{:S(2)}) copy-start(s32[1,256]{1,0:T(1,128)} %param.8) | copy-start | bytes 3076
  26.3 121.1 %copy-start = (bf16[1,64,512]{2,1,0:T(8,128)(2,1)S(1)}, bf16[1,64,512]{2,1,0:T(8,128)(2,1)}, u32[]{:S(2)}) copy-start(bf16[1,64,512]{2,1,0:T(8,128)(2,1)} %param.7) | copy-start | bytes 196612
  26.3 126.4 %copy-start.2 = (s32[1,9]{1,0:T(1,128)S(1)}, s32[1,9]{1,0:T(1,128)}, u32[]{:S(2)}) copy-start(s32[1,9]{1,0:T(1,128)} %param.9) | copy-start | bytes 112
  26.3 165.7 %all-to-all-start = ((bf16[8,64,4608]{2,1,0:T(8,128)(2,1)}), bf16[8,64,4608]{2,1,0:T(8,128)(2,1)}, u32[]{:S(2)}, u32[]{:S(2)}) async-start(bf16[8,64,4608]{2,1,0:T(8,128)(2,1)} %stack.2), calls=%async_computation | async-start | bytes 9437184 | tf_op jit(solution)/shard_map/all_to_all | solution.py:47
  145.4 44.6 %collective-permute-start = (bf16[512,512]{0,1:T(8,128)(2,1)S(1)}, bf16[512,512]{0,1:T(8,128)(2,1)S(1)}, u32[]{:S(2)}, u32[]{:S(2)}) collective-permute-start(bf16[512,512]{0,1:T(8,128)(2,1)S(1)} %copy.17), channel_id=1, source_target_pairs={{0,32},{8,40},{16,48},{24,56},{32,0},{40,8},{48,16},{56,24},{64,96... | collective-permute-start | bytes 1572872 | tf_op jit(solution)/shard_map/ppermute | solution.py:11
Sparse Core Ops, SparseCore 0:
  9.6 117.3 all-gather.1
